TPU v7x, 512 devices: a whole 4x8x8 slice. The times are simulated.
512 devices in a mesh: dp: 16 (over y, core), expert: 8 (over z), tensor: 4 (over x).
Axes of the slice: x: 4, y: 8, z: 8, core: 2. Of those that a mesh axis runs over, the one named last changes fastest.
Arguments:
- tokens: bfloat16 [8192, 4096], P(('dp', 'expert'), 'tensor'), may hold values from -6 to 6
- expert_ids: int32 [8192, 8], P(('dp', 'expert')), may hold values from 0 to 127, all different within a row; in each aligned block of 64 rows (0 to 63, 64 to 127, ...) at most 6 rows name the same one
- combine_weights: float32 [8192, 8], P(('dp', 'expert')), may hold values from 0.05 to 1
- topology: int32 [128, 12, 12], P(('dp', 'expert'), 'tensor'), may hold values from 0 to 31, all different within a row
- gate_blocks: bfloat16 [128, 12, 12, 128, 128], P(('dp', 'expert'), 'tensor'), may hold values from -0.15625 to 0.15625
- up_blocks: bfloat16 [128, 12, 12, 128, 128], P(('dp', 'expert'), 'tensor'), may hold values from -0.15625 to 0.15625
- down_blocks: bfloat16 [128, 12, 12, 128, 128], P(('dp', 'expert'), 'tensor'), may hold values from -0.25 to 0.25
Outputs:
- layer_out: bfloat16 [8192, 4096], P(('dp', 'expert'), 'tensor')
Inputs may be any that keep to these rules, and one draw needn't show every extreme that they name: `expert_ids`: in each aligned block of 64 tokens (the tokens of one index of dp+expert), no expert is named more than 6 times, a bound that some block reaches; a token names 8 different experts. `topology`: each row names 12 different blocks; every block is named by some row.
All inputs are finite; a program needn't handle non-finite values.
Results may differ from a plain program's by a relative error of at most 0.0058.
Values may be sent and summed in bfloat16 or wider, within the bound.
A program may use at most 128 MiB of HBM per device.

v0:
```python
import jax
import jax.numpy as jnp
from jax import lax
from jax.sharding import PartitionSpec as P

D = 4096
TOP = 8
BLK = 128


def slot_numbers(expert_ids, experts):
    flat_ids = expert_ids.reshape(-1)
    onehot = (flat_ids[:, None] == jnp.arange(experts, dtype=jnp.int32)[None, :]).astype(jnp.int32)
    before = jnp.cumsum(onehot, axis=0) - onehot
    return jnp.sum(before * onehot, axis=1).reshape(expert_ids.shape)


def combine_rows(flat_rows, target, combine_weights):
    total = jnp.zeros((target.shape[0], flat_rows.shape[1]), jnp.float32)
    for pick in range(target.shape[1]):
        chosen = jnp.take(flat_rows, target[:, pick], axis=0)
        total = total + combine_weights[:, pick][:, None] * chosen
    return total


def per_device(tokens, expert_ids, combine_weights, topology, gate_blocks, up_blocks, down_blocks):
    experts = lax.axis_size(("dp", "expert"))
    tok_rows = tokens.shape[0]
    capacity = min(tok_rows, 3 * tok_rows * TOP // (2 * experts))
    slot_index = slot_numbers(expert_ids, experts)
    target = expert_ids * capacity + slot_index
    places = jnp.arange(experts * capacity, dtype=jnp.int32)
    matches = target[None, :, :] == places[:, None, None]
    dispatch = jnp.any(matches, axis=2).astype(jnp.bfloat16)
    outgoing = jnp.dot(dispatch, tokens, preferred_element_type=jnp.float32).astype(jnp.bfloat16)
    outgoing = outgoing.reshape(experts, capacity, tokens.shape[1])
    arrived = lax.all_to_all(outgoing, ("dp", "expert"), split_axis=0, concat_axis=0, tiled=True)
    expert_in = lax.all_gather(arrived, "tensor", axis=2, tiled=True)
    row_count = experts * capacity
    layout_ids = topology[0]
    local_blocks = layout_ids.shape[0]
    blocked = expert_in.reshape(row_count, D // BLK, BLK)
    width_ids = jnp.arange(D // BLK, dtype=jnp.int32)
    partial_value = jnp.zeros((row_count, D // BLK, BLK), jnp.float32)
    for block in range(local_blocks):
        chosen = layout_ids[block]
        picked = jnp.take(blocked, chosen, axis=1)
        gate_proj = jnp.einsum(
            "rkc,kcf->rf", picked, gate_blocks[0, block], preferred_element_type=jnp.float32
        )
        up_proj = jnp.einsum(
            "rkc,kcf->rf", picked, up_blocks[0, block], preferred_element_type=jnp.float32
        )
        hidden = (jax.nn.silu(gate_proj) * up_proj).astype(jnp.bfloat16)
        pieces = jnp.einsum(
            "rf,kfc->rkc", hidden, down_blocks[0, block], preferred_element_type=jnp.float32
        )
        placer = (chosen[:, None] == width_ids[None, :]).astype(jnp.float32)
        partial_value = partial_value + jnp.einsum(
            "rkc,kb->rbc", pieces, placer, precision=lax.Precision.HIGHEST
        )
    partial_low = lax.optimization_barrier(
        partial_value.reshape(experts, capacity, D).astype(jnp.bfloat16)
    )
    shares = lax.all_to_all(
        partial_low.reshape(1, experts, capacity, D),
        "tensor",
        split_axis=3,
        concat_axis=0,
        tiled=True,
    )
    summed = jnp.sum(shares.astype(jnp.float32), axis=0)
    returned_rows = lax.all_to_all(
        summed, ("dp", "expert"), split_axis=0, concat_axis=0, tiled=True
    )
    flat_rows = returned_rows.reshape(row_count, returned_rows.shape[2])
    combined = combine_rows(flat_rows, target, combine_weights)
    return combined.astype(jnp.bfloat16)


def solution(mesh):
    return jax.shard_map(
        per_device,
        mesh=mesh,
        in_specs=(
            P(("dp", "expert"), "tensor"),
            P(("dp", "expert"), None),
            P(("dp", "expert"), None),
            P(("dp", "expert"), "tensor", None),
            P(("dp", "expert"), "tensor", None, None, None),
            P(("dp", "expert"), "tensor", None, None, None),
            P(("dp", "expert"), "tensor", None, None, None),
        ),
        out_specs=P(("dp", "expert"), "tensor"),
        check_vma=False,
    )
```

profile of v0, /device:TPU:1, one launch (start us, length us, event | category | flops | bytes accessed | tf_op | source)
XLA Modules:
  0.0 545.4 jit_solution(15346772995551788982)
XLA Ops:
  9.7 1.8 convolution_convert_fusion
  11.5 2.5 reshape.63
  14.0 73.0 %all_to_all.19 = bf16[128,6,1024]{2,1,0:T(8,128)(2,1)} all-to-all(bf16[128,6,1024]{2,1,0:T(8,128)(2,1)S(1)} %reshape.63), channel_id=1, replica_groups=mesh['dp'=16,'expert'=8,'tensor'=4] {'dp','expert'}, dimensions={0} | all-to-all | bytes 3145728 | tf_op jit(solution)/shard_map/all_to_all | solution.py:37
  87.0 81.0 %all-gather.2.cloned.1.call-done = bf16[128,6,4096]{2,1,0:T(8,128)(2,1)} async-done(((bf16[128,6,1024]{2,1,0:T(8,128)(2,1)}), bf16[128,6,4096]{2,1,0:T(8,128)(2,1)}) %all-gather.2.cloned.1.call-update) | async-done | bytes 6291472 | tf_op jit(solution)/shard_map/all_gather | solution.py:38
  168.1 13.8 %reshape.64 = bf16[768,32,128]{2,1,0:T(8,128)(2,1)} reshape(bf16[128,6,4096]{2,1,0:T(8,128)(2,1)} %all-gather.2.cloned.1.call-done) | data formatting | bytes 12582912 | tf_op jit(solution)/shard_map/reshape | solution.py:42
  181.9 7.9 %copy.83 = bf16[768,32,128]{2,0,1:T(8,128)(2,1)} copy(bf16[768,32,128]{2,1,0:T(8,128)(2,1)} %reshape.64) | data formatting | bytes 12582912 | tf_op jit(solution)/shard_map/reshape | solution.py:42
  189.7 5.2 gather_fusion.1
  194.9 3.8 gather_fusion.2
  198.7 2.5 fusion.28
  201.2 1.8 fusion.34
  203.0 6.5 %fusion.71 = f32[768,12,128]{2,0,1:T(8,128)} fusion(bf16[12,768,128]{2,1,0:T(8,128)(2,1)} %gather_fusion.1, pred[12]{0:T(512)(128)(4,1)S(1)} %get-tuple-element.56, bf16[1,3,12,128,128]{4,3,2,1,0:T(8,128)(2,1)} %param.17, bf16[1,3,12,128,128]{4,3,2,1,0:T(8,128)(2,1)} %param.16, f32[768,128]{1,0:T(8,128)S(1)} %fusion.28), kind=kOutput, calls=%fused_computation.54 | convolution fusion | flops 605749248 | bytes 8257548 | tf_op jit(solution)/shard_map/rf,kfc->rkc/dot_general | solution.py:55
  209.5 5.8 %fusion.74 = f32[768,12,128]{2,0,1:T(8,128)} fusion(bf16[12,768,128]{2,1,0:T(8,128)(2,1)S(1)} %gather_fusion.2, pred[12]{0:T(512)(128)(4,1)S(1)} %get-tuple-element.54, bf16[1,3,12,128,128]{4,3,2,1,0:T(8,128)(2,1)} %param.17, bf16[1,3,12,128,128]{4,3,2,1,0:T(8,128)(2,1)} %param.16, f32[768,128]{1,0:T(8,128)S(1)} %fusion.34), kind=kOutput, calls=%fused_computation.55 | convolution fusion | flops 605749248 | bytes 8257548 | tf_op jit(solution)/shard_map/rf,kfc->rkc/dot_general | solution.py:55
  215.3 3.8 gather_fusion
  219.1 1.4 copy-done.2
  220.5 1.8 fusion.22
  222.3 6.6 %fusion.68 = f32[768,12,128]{2,0,1:T(8,128)} fusion(bf16[12,768,128]{2,1,0:T(8,128)(2,1)} %copy-done.2, pred[12]{0:T(512)(128)(4,1)S(1)} %get-tuple-element.23, bf16[1,3,12,128,128]{4,3,2,1,0:T(8,128)(2,1)} %param.17, bf16[1,3,12,128,128]{4,3,2,1,0:T(8,128)(2,1)} %param.16, f32[768,128]{1,0:T(8,128)S(1)} %fusion.22), kind=kOutput, calls=%fused_computation.53 | convolution fusion | flops 605749248 | bytes 8257548 | tf_op jit(solution)/shard_map/rf,kfc->rkc/dot_general | solution.py:55
  229.0 13.8 %fusion.3 = f32[32,768,128]{2,0,1:T(8,128)} fusion(f32[768,12,128]{2,0,1:T(8,128)} %fusion.71, s32[12]{0:T(128)S(1)} %get-tuple-element.53), kind=kOutput, calls=%fused_computation.16 | convolution fusion | flops 452985216 | bytes 17301552 | tf_op jit(solution)/shard_map/rkc,kb->rbc/dot_general | solution.py:59
  242.7 12.7 %fusion.1 = f32[32,768,128]{2,0,1:T(8,128)} fusion(f32[768,12,128]{2,0,1:T(8,128)S(1)} %bitcast.217, s32[12]{0:T(128)S(1)} %get-tuple-element.52), kind=kOutput, calls=%fused_computation.14 | convolution fusion | flops 452985216 | bytes 17301552 | tf_op jit(solution)/shard_map/rkc,kb->rbc/dot_general | solution.py:59
  255.5 17.1 %fusion = bf16[768,32,128]{2,1,0:T(8,128)(2,1)} fusion(f32[32,768,128]{2,0,1:T(8,128)} %fusion.1, f32[32,768,128]{2,0,1:T(8,128)} %fusion.3, f32[768,12,128]{2,0,1:T(8,128)S(1)} %bitcast.215, s32[12]{0:T(128)S(1)} %get-tuple-element.51), kind=kOutput, calls=%fused_computation.13 | convolution fusion | flops 462422400 | bytes 36175920 | tf_op jit(solution)/shard_map/rkc,kb->rbc/dot_general | solution.py:59
  272.6 13.3 %convert_element_type.51 = bf16[128,6,4096]{2,1,0:T(8,128)(2,1)} reshape(bf16[768,32,128]{2,1,0:T(8,128)(2,1)} %fusion) | data formatting | bytes 12582912 | tf_op jit(solution)/shard_map/convert_element_type | solution.py:63
  285.9 12.8 %copy.89 = bf16[1,128,6,4096]{1,2,0,3:T(8,128)(2,1)} copy(bf16[1,128,6,4096]{3,2,1,0:T(8,128)(2,1)} %bitcast.213) | data formatting | bytes 12582912 | tf_op jit(solution)/shard_map/reshape | solution.py:66
  298.7 96.9 %all_to_all.20 = bf16[1,128,6,4096]{1,2,0,3:T(8,128)(2,1)S(1)} all-to-all(bf16[1,128,6,4096]{1,2,0,3:T(8,128)(2,1)} %copy.89), channel_id=1, replica_groups=mesh['dp'=16,'expert'=8,'tensor'=4] {'tensor'}, dimensions={3} | all-to-all | bytes 12582912 | tf_op jit(solution)/shard_map/all_to_all | solution.py:65
  395.6 3.5 copy.90
  399.1 4.1 convert_reduce_fusion
  403.1 3.5 copy.91
  406.6 16.1 %all-to-all-start.2 = ((f32[128,6,1024]{2,1,0:T(8,128)}), f32[128,6,1024]{2,1,0:T(8,128)}, u32[]{:S(2)}, u32[]{:S(2)}) async-start(f32[128,6,1024]{2,1,0:T(8,128)} %copy.91), calls=%async_computation.2 | async-start | bytes 8388608 | tf_op jit(solution)/shard_map/all_to_all | solution.py:73
  424.0 98.6 %all-to-all-done.2 = f32[128,6,1024]{2,1,0:T(8,128)} async-done(((f32[128,6,1024]{2,1,0:T(8,128)}), f32[128,6,1024]{2,1,0:T(8,128)}, u32[]{:S(2)}, u32[]{:S(2)}) %all-to-all-start.2) | async-done | bytes 3145760 | tf_op jit(solution)/shard_map/all_to_all | solution.py:73
  522.6 3.1 reshape.66
  526.3 1.4 gather_fusion.4
  529.1 1.4 gather_fusion.6
  530.4 1.4 gather_fusion.7
  535.9 2.4 fusion.118
  (55 shorter events, 10.5 us)
Async XLA Ops:
  6.5 3.2 copy-start
  6.5 161.6 %all-gather.2.cloned.1.call-start = ((), (), s32[]{:S(2)}) async-start(), calls=%async_computation.3 | async-start | bytes 10485760 | tf_op jit(solution)/shard_map/all_gather | solution.py:38
  14.0 73.0 %copy-start.3 = (s32[1,3,12]{2,0,1:T(1,128)S(1)}, s32[1,3,12]{2,0,1:T(1,128)}, u32[]{:S(2)}) copy-start(s32[1,3,12]{2,0,1:T(1,128)} %param.14) | copy-start | bytes 436
  219.1 1.4 copy-start.2
  222.3 20.4 %slice-start.2 = ((s8[4718592]{0:T(1024)(128)(4,1)}), s8[524288]{0:T(1024)(128)(4,1)S(1)}, s32[]{:S(2)}) async-start(s8[4718592]{0:T(1024)(128)(4,1)} %bitcast.216), calls=%async_computation.6 | async-start | bytes 1048576
  228.9 13.8 %slice-start.3 = ((s8[4718592]{0:T(1024)(128)(4,1)}), s8[4194304]{0:T(1024)(128)(4,1)S(1)}, s32[]{:S(2)}) async-start(s8[4718592]{0:T(1024)(128)(4,1)} %bitcast.216), calls=%async_computation.7 | async-start | bytes 8388608
  229.0 26.5 %slice-start = ((s8[4718592]{0:T(1024)(128)(4,1)}), s8[4194304]{0:T(1024)(128)(4,1)S(1)}, s32[]{:S(2)}) async-start(s8[4718592]{0:T(1024)(128)(4,1)} %bitcast.214), calls=%async_computation.4 | async-start | bytes 8388608
  242.7 12.8 %slice-start.1 = ((s8[4718592]{0:T(1024)(128)(4,1)}), s8[524288]{0:T(1024)(128)(4,1)S(1)}, s32[]{:S(2)}) async-start(s8[4718592]{0:T(1024)(128)(4,1)} %bitcast.214), calls=%async_computation.5 | async-start | bytes 1048576
  406.6 16.8 %copy-start.4 = (f32[64,8]{0,1:T(8,128)S(1)}, f32[64,8]{0,1:T(8,128)}, u32[]{:S(2)}) copy-start(f32[64,8]{0,1:T(8,128)} %param.13) | copy-start | bytes 6148
  406.6 116.0 %all-to-all-start.2 = ((f32[128,6,1024]{2,1,0:T(8,128)}), f32[128,6,1024]{2,1,0:T(8,128)}, u32[]{:S(2)}, u32[]{:S(2)}) async-start(f32[128,6,1024]{2,1,0:T(8,128)} %copy.91), calls=%async_computation.2 | async-start | bytes 8388608 | tf_op jit(solution)/shard_map/all_to_all | solution.py:73
  533.2 5.1 copy-start.1
  534.6 1.4 copy-start.5
Sparse Core Ops, SparseCore 0:
  87.1 80.9 all-gather.1
where the time goes:
time: 550 us; the launch traced here: 545 us
  waiting for transfers between devices  180 us (33%)
  blocking collectives  170 us (31%)
  local copies, waits for them, and re-layouts  86.6 us (16%)
  matrix products  70.4 us (13%)
  starting transfers between devices  16.1 us (3%)
  between operations  13.9 us (3%)
  other arithmetic  8.84 us (2%)
    all_to_all x1, waiting for transfers between devices, per_device(): lax.all_to_all(summed, ('dp', 'expert'), split_axis=0, concat_axis=0, til...  98.6 us
    all_to_all x1, blocking collectives, per_device(): lax.all_to_all(partial_low.reshape(1, experts, capacity, D), 'tensor', sp...  96.9 us
    all_gather x1, waiting for transfers between devices, per_device(): expert_in = lax.all_gather(arrived, 'tensor', axis=2, tiled=True)  81 us
    all_to_all x1, blocking collectives, per_device(): lax.all_to_all(outgoing, ('dp', 'expert'), split_axis=0, concat_axis=0, t...  73 us
    dot_general x3, matrix products, per_device(): jnp.einsum('rkc,kb->rbc', pieces, placer, precision=lax.Precision.HIGHEST)  43.6 us
    reshape x2, local copies, waits for them, and re-layouts, per_device(): blocked = expert_in.reshape(row_count, D // BLK, BLK)  21.6 us
    dot_general x3, matrix products, per_device(): jnp.einsum('rf,kfc->rkc', hidden, down_blocks[0, block], preferred_elemen...  18.9 us
    all_to_all x1, starting transfers between devices, per_device(): lax.all_to_all(summed, ('dp', 'expert'), split_axis=0, concat_axis=0, til...  16.1 us
  transfers between devices with their start and end apart: 2, of which 2 were waited for; matrix products, arithmetic and copies ran while one was open for 0% of the time, Pallas kernels for 0%

commit v1 on v0

v1 whole, which is shorter than its diff:
```python
import functools

import jax
import jax.numpy as jnp
from jax import lax
from jax.experimental import pallas as pl
from jax.experimental.pallas import tpu as pltpu
from jax.sharding import PartitionSpec as P

BLK = 128
PIECES = 4
F32, BF16 = jnp.float32, jnp.bfloat16
MESH = pl.DeviceIdType.MESH


def matmul(a, b):
    return jnp.dot(a, b, preferred_element_type=F32)


def layer_kernel(cfg, tok, ids, wts, inv, gate, up, down, out, *scratch):
    n_dp, n_z, n_x, cap, toks, width, kb, hb = cfg
    (gbuf, ubuf, dbuf, gu, dn, tabs_out, tabs, tokp, zbuf, qa, va, disp, ct, comb_hi, comb_lo, ysend, xin, acc, hid,
     asend, arecv, bsend_r, bsend_l, brecv_l, brecv_r, fsend, yret, gsend, zret,
     w_sem, t_send, t_recv, z_send, z_recv, y_send, y_recv, r1_send, l1_send, r1_recv, l1_recv, r2_send, l2_send,
     r2_recv, l2_recv, ar_send, al_send, ar_recv, al_recv, br_send, bl_send, br_recv, bl_recv,
     f_send, f_recv, g_send, g_recv) = scratch
    pieces = xin.shape[1]
    w = width // pieces
    grp = n_z * cap
    rows = n_dp * grp
    half = rows // 2
    all_tok = n_z * toks
    hid_w = hb * BLK
    per = w // BLK
    dp, z, x = lax.axis_index("dp"), lax.axis_index("expert"), lax.axis_index("tensor")
    right, left, far = lax.rem(x + 1, n_x), lax.rem(x + n_x - 1, n_x), lax.rem(x + 2, n_x)

    def remote(src, dst, ssem, rsem, where):
        return pltpu.make_async_remote_copy(
            src_ref=src, dst_ref=dst, send_sem=ssem, recv_sem=rsem, device_id=where, device_id_type=MESH)

    def drain(ref, sem):
        pltpu.make_async_copy(ref, ref, sem).wait()

    weight_copies = [
        pltpu.make_async_copy(src.at[0], buf.at[:, pl.ds(0, kb)], w_sem.at[i])
        for i, (src, buf) in enumerate(((gate, gbuf), (up, ubuf), (down, dbuf)))
    ]
    for c in weight_copies:
        c.start()

    barrier = pltpu.get_barrier_semaphore()

    def greet_dp(i, _):
        pl.semaphore_signal(barrier, inc=1, device_id={"dp": lax.rem(dp + i, n_dp)}, device_id_type=MESH)
        return 0

    def greet_z(i, _):
        pl.semaphore_signal(barrier, inc=1, device_id={"expert": lax.rem(z + i, n_z)}, device_id_type=MESH)
        return 0

    lax.fori_loop(1, n_dp, greet_dp, 0)
    lax.fori_loop(1, n_z, greet_z, 0)
    pl.semaphore_signal(barrier, inc=1, device_id={"tensor": right}, device_id_type=MESH)
    pl.semaphore_signal(barrier, inc=1, device_id={"tensor": left}, device_id_type=MESH)

    n_e = n_z * n_dp
    q = lax.broadcasted_iota(jnp.int32, (n_e, 2 * toks), 0)
    lane = lax.broadcasted_iota(jnp.int32, (n_e, 2 * toks), 1)
    shift = n_dp.bit_length() - 1
    expert = (q & (n_dp - 1)) * n_z + (q >> shift)
    named = jnp.zeros((n_e, 2 * toks), F32)
    weight = jnp.zeros((n_e, 2 * toks), F32)
    for k in range(ids.shape[0]):
        same = ids[k : k + 1, :] == expert
        named = named + jnp.where(same, 1.0, 0.0)
        weight = weight + jnp.where(same, wts[k : k + 1, :], 0.0)
    before = lax.broadcasted_iota(jnp.int32, (2 * toks, 2 * toks), 0)
    after = lax.broadcasted_iota(jnp.int32, (2 * toks, 2 * toks), 1) & (toks - 1)
    earlier = jnp.where((before < after) & (before < toks), 1.0, 0.0).astype(BF16)
    slot = matmul(named.astype(BF16), earlier)
    table = jnp.where(lane < toks, jnp.where(named > 0.5, slot, -1.0), weight)
    tabs_out[...] = table.reshape(n_z, n_dp, 2 * toks)
    for p in range(pieces):
        tokp[p] = tok[:, p * w : (p + 1) * w]

    pl.semaphore_wait(barrier, (n_dp - 1) + (n_z - 1) + 2)

    def send_table(i, _):
        to = lax.rem(z + i, n_z)
        remote(tabs_out.at[to], tabs.at[z], t_send, t_recv, {"expert": to}).start()
        return 0

    lax.fori_loop(1, n_z, send_table, 0)

    def send_tokens(j, _):
        p, i = j // (n_z - 1), lax.rem(j, n_z - 1) + 1
        remote(tokp.at[p], zbuf.at[p, z], z_send.at[p], z_recv.at[p], {"expert": lax.rem(z + i, n_z)}).start()
        return 0

    lax.fori_loop(0, pieces * (n_z - 1), send_tokens, 0)
    tabs[z] = tabs_out[z]
    for p in range(pieces):
        zbuf[p, z] = tokp[p]

    for buf in (gbuf, ubuf, dbuf):
        buf[:, kb] = jnp.zeros((hb, BLK, BLK), BF16)
    acc[...] = jnp.zeros(acc.shape, F32)
    for c in weight_copies:
        c.wait()

    def dense(i, _):
        for j in range(per):
            b = i * per + j
            for h in range(hb):
                at = inv[h, b]
                gu[i, j * BLK : (j + 1) * BLK, h * BLK : (h + 1) * BLK] = gbuf[h, at]
                gu[i, j * BLK : (j + 1) * BLK, hid_w + h * BLK : hid_w + (h + 1) * BLK] = ubuf[h, at]
                dn[i, h * BLK : (h + 1) * BLK, j * BLK : (j + 1) * BLK] = dbuf[h, at]
        return 0

    lax.fori_loop(0, n_x * pieces, dense, 0)

    drain(tabs.at[pl.ds(0, n_z - 1)], t_recv)
    low = lax.broadcasted_iota(jnp.int32, (n_dp, 2 * toks), 1) < toks
    for j in range(n_z // 2):
        one, two = tabs[2 * j], tabs[2 * j + 1]
        qa[:, j * 2 * toks : (j + 1) * 2 * toks] = jnp.where(low, one, pltpu.roll(two, toks, 1))
        va[:, j * 2 * toks : (j + 1) * 2 * toks] = jnp.where(low, pltpu.roll(one, toks, 1), two)
    r = lax.broadcasted_iota(jnp.int32, (grp, all_tok), 0)
    home = jnp.zeros((grp, all_tok), jnp.int32)
    for j in range(1, n_z):
        home = home + jnp.where(r >= cap * j, 1, 0)
    home_of_token = lax.broadcasted_iota(jnp.int32, (grp, all_tok), 1) >> (toks.bit_length() - 1)
    wanted = jnp.where(home == home_of_token, r - cap * home, -2).astype(F32)

    def one_hot(d, _):
        hit = jnp.broadcast_to(qa[pl.ds(d, 1), :], (grp, all_tok)) == wanted
        at = pl.ds(pl.multiple_of(d * grp, grp), grp)
        disp[at, :] = jnp.where(hit, 1.0, 0.0).astype(BF16)
        ct[at, :] = jnp.where(hit, jnp.broadcast_to(va[pl.ds(d, 1), :], (grp, all_tok)), 0.0)
        return 0

    lax.fori_loop(0, n_dp, one_hot, 0)

    third = rows // 3

    def gather_piece(p):
        drain(zbuf.at[p, pl.ds(0, n_z - 1)], z_recv.at[p])
        t = zbuf[p].reshape(all_tok, w)

        def tile(i, _):
            at = pl.ds(pl.multiple_of(i * third, 16), third)
            ysend[p, at, :] = matmul(disp[at, :], t).astype(BF16)
            return 0

        lax.fori_loop(0, 3, tile, 0)
        mine = pl.ds(pl.multiple_of(dp * grp, 16), grp)

        def send(i, _):
            to = lax.rem(dp + i, n_dp)
            remote(ysend.at[p, pl.ds(pl.multiple_of(to * grp, 16), grp)], xin.at[x, p, mine],
                   y_send.at[p], y_recv.at[p], {"dp": to}).start()
            return 0

        lax.fori_loop(1, n_dp, send, 0)
        xin[x, p, mine, :] = ysend[p, mine, :]

    def spread_piece(p):
        drain(xin.at[x, p, pl.ds(0, rows - grp)], y_recv.at[p])
        src = xin.at[x, p]
        remote(src, src, r1_send.at[p], r1_recv.at[p], {"tensor": right}).start()
        remote(src, src, l1_send.at[p], l1_recv.at[p], {"tensor": left}).start()

    def forward_piece(p):
        drain(xin.at[left, p], r1_recv.at[p])
        src = xin.at[left, p, pl.ds(0, half)]
        remote(src, src, r2_send.at[p], r2_recv.at[p], {"tensor": right}).start()
        drain(xin.at[right, p], l1_recv.at[p])
        src = xin.at[right, p, pl.ds(half, half)]
        remote(src, src, l2_send.at[p], l2_recv.at[p], {"tensor": left}).start()

    def add_piece(quarter, p):
        def tile(i, _):
            at = pl.ds(pl.multiple_of(i * third, 16), third)
            acc[at, :] += matmul(xin[quarter, p, at, :], gu[quarter * pieces + p])
            return 0

        lax.fori_loop(0, 3, tile, 0)

    def inward(t, _):
        @pl.when(t < pieces)
        def _():
            gather_piece(t)

        @pl.when((t >= 1) & (t < pieces + 1))
        def _():
            spread_piece(t - 1)

        @pl.when((t >= 2) & (t < pieces + 2))
        def _():
            forward_piece(t - 2)
            add_piece(x, t - 2)
            add_piece(left, t - 2)
            add_piece(right, t - 2)

        @pl.when(t >= 3)
        def _():
            drain(xin.at[far, t - 3, pl.ds(0, half)], r2_recv.at[t - 3])
            drain(xin.at[far, t - 3, pl.ds(half, half)], l2_recv.at[t - 3])
            add_piece(far, t - 3)

        return 0

    tr = min(rows, BLK)
    for j in range(rows // tr):
        c = ct[j * tr : (j + 1) * tr, :].T
        hi = c.astype(BF16)
        comb_hi[:, j * tr : (j + 1) * tr] = hi
        comb_lo[:, j * tr : (j + 1) * tr] = (c - hi.astype(F32)).astype(BF16)

    lax.fori_loop(0, pieces + 3, inward, 0)

    def activate(i, _):
        at = pl.ds(pl.multiple_of(i * third, 16), third)
        g = acc[at, :hid_w]
        hid[at, :] = (g / (1.0 + jnp.exp(-g)) * acc[at, hid_w:]).astype(BF16)
        return 0

    lax.fori_loop(0, 3, activate, 0)

    def partial(quarter, p, part):
        return matmul(hid[part * half : (part + 1) * half, :], dn[quarter * pieces + p])

    lo, hi_ = pl.ds(0, half), pl.ds(half, half)

    def send_far(p):
        asend[p, lo, :] = partial(far, p, 0).astype(BF16)
        remote(asend.at[p, lo], arecv.at[p, lo], ar_send.at[p], ar_recv.at[p], {"tensor": right}).start()
        asend[p, hi_, :] = partial(far, p, 1).astype(BF16)
        remote(asend.at[p, hi_], arecv.at[p, hi_], al_send.at[p], al_recv.at[p], {"tensor": left}).start()

    def send_near(p):
        bsend_r[p, hi_, :] = partial(right, p, 1).astype(BF16)
        bsend_l[p, lo, :] = partial(left, p, 0).astype(BF16)
        drain(arecv.at[p, lo], ar_recv.at[p])
        bsend_r[p, lo, :] = (partial(right, p, 0) + arecv[p, lo, :].astype(F32)).astype(BF16)
        remote(bsend_r.at[p], brecv_l.at[p], br_send.at[p], br_recv.at[p], {"tensor": right}).start()
        drain(arecv.at[p, hi_], al_recv.at[p])
        bsend_l[p, hi_, :] = (partial(left, p, 1) + arecv[p, hi_, :].astype(F32)).astype(BF16)
        remote(bsend_l.at[p], brecv_r.at[p], bl_send.at[p], bl_recv.at[p], {"tensor": left}).start()

    def send_home(p):
        drain(brecv_l.at[p], br_recv.at[p])
        drain(brecv_r.at[p], bl_recv.at[p])
        for part, at in ((0, lo), (1, hi_)):
            total = partial(x, p, part) + brecv_l[p, at, :].astype(F32) + brecv_r[p, at, :].astype(F32)
            fsend[p, at, :] = total.astype(BF16)
        mine = pl.ds(pl.multiple_of(dp * grp, 16), grp)

        def send(i, _):
            to = lax.rem(dp + i, n_dp)
            remote(fsend.at[p, pl.ds(pl.multiple_of(to * grp, 16), grp)], yret.at[p, mine],
                   f_send.at[p], f_recv.at[p], {"dp": to}).start()
            return 0

        lax.fori_loop(1, n_dp, send, 0)
        yret[p, mine, :] = fsend[p, mine, :]

    def combine(p):
        drain(yret.at[p, pl.ds(0, rows - grp)], f_recv.at[p])

        def tile(i, _):
            at = pl.ds(pl.multiple_of(i * 2 * toks, 2 * toks), 2 * toks)
            s = matmul(comb_hi[at, :], yret[p]) + matmul(comb_lo[at, :], yret[p])
            gsend[p, pl.ds(2 * i, 2)] = s.astype(BF16).reshape(2, toks, w)
            return 0

        lax.fori_loop(0, n_z // 2, tile, 0)

        def send(i, _):
            to = lax.rem(z + i, n_z)
            remote(gsend.at[p, to], zret.at[p, z], g_send.at[p], g_recv.at[p], {"expert": to}).start()
            return 0

        lax.fori_loop(1, n_z, send, 0)
        zret[p, z] = gsend[p, z]

    def finish(p):
        drain(zret.at[p, pl.ds(0, n_z - 1)], g_recv.at[p])
        total = zret[p, 0].astype(F32)
        for h in range(1, n_z):
            total = total + zret[p, h].astype(F32)
        out[:, pl.ds(pl.multiple_of(p * w, BLK), w)] = total.astype(BF16)

    send_far(0)
    send_far(1)

    def outward(t, _):
        @pl.when(t < pieces)
        def _():
            send_near(t)

        @pl.when(t + 2 < pieces)
        def _():
            send_far(t + 2)

        @pl.when((t >= 1) & (t < pieces + 1))
        def _():
            send_home(t - 1)

        @pl.when((t >= 2) & (t < pieces + 2))
        def _():
            combine(t - 2)

        @pl.when(t >= 3)
        def _():
            finish(t - 3)

        return 0

    lax.fori_loop(0, pieces + 3, outward, 0)

    drain(tabs_out.at[pl.ds(0, n_z - 1)], t_send)

    def settle(p, _):
        drain(zbuf.at[p, pl.ds(0, n_z - 1)], z_send.at[p])
        drain(ysend.at[p, pl.ds(0, rows - grp)], y_send.at[p])
        drain(xin.at[0, p], r1_send.at[p])
        drain(xin.at[0, p], l1_send.at[p])
        drain(xin.at[0, p, lo], r2_send.at[p])
        drain(xin.at[0, p, lo], l2_send.at[p])
        drain(asend.at[p, lo], ar_send.at[p])
        drain(asend.at[p, lo], al_send.at[p])
        drain(bsend_r.at[p], br_send.at[p])
        drain(bsend_l.at[p], bl_send.at[p])
        drain(fsend.at[p, pl.ds(0, rows - grp)], f_send.at[p])
        drain(gsend.at[p, pl.ds(0, n_z - 1)], g_send.at[p])
        return 0

    lax.fori_loop(0, pieces, settle, 0)


def per_device(tokens, expert_ids, combine_weights, topology, gate_blocks, up_blocks, down_blocks):
    n_dp, n_z, n_x = (lax.axis_size(a) for a in ("dp", "expert", "tensor"))
    toks, width = tokens.shape
    top = expert_ids.shape[1]
    cap = min(toks, 3 * toks * top // (2 * n_dp * n_z))
    _, hb, kb = topology.shape
    n_b = n_x * width // BLK
    pieces, w = PIECES, width // PIECES
    rows, grp = n_dp * n_z * cap, n_z * cap
    ids = jnp.concatenate([expert_ids.T, expert_ids.T], axis=1)
    wts = jnp.concatenate([combine_weights.T, combine_weights.T], axis=1)
    hits = topology[0][:, :, None] == jnp.arange(n_b, dtype=jnp.int32)[None, None, :]
    inv = kb + jnp.sum(jnp.where(hits, jnp.arange(kb, dtype=jnp.int32)[None, :, None] - kb, 0), axis=1)
    vm, dma = pltpu.VMEM, pltpu.SemaphoreType.DMA
    hid_w = hb * BLK
    scratch = (
        [vm((hb, kb + 1, BLK, BLK), BF16)] * 3
        + [
            vm((n_x * pieces, w, 2 * hid_w), BF16),
            vm((n_x * pieces, hid_w, w), BF16),
            vm((n_z, n_dp, 2 * toks), F32),
            vm((n_z, n_dp, 2 * toks), F32),
            vm((pieces, toks, w), BF16),
            vm((pieces, n_z, toks, w), BF16),
            vm((n_dp, n_z * toks), F32),
            vm((n_dp, n_z * toks), F32),
            vm((rows, n_z * toks), BF16),
            vm((rows, n_z * toks), F32),
            vm((n_z * toks, rows), BF16),
            vm((n_z * toks, rows), BF16),
            vm((pieces, rows, w), BF16),
            vm((n_x, pieces, rows, w), BF16),
            vm((rows, 2 * hid_w), F32),
            vm((rows, hid_w), BF16),
        ]
        + [vm((pieces, rows, w), BF16)] * 8
        + [vm((pieces, n_z, toks, w), BF16)] * 2
        + [dma((3,)), dma(()), dma(())]
        + [dma((pieces,))] * 24
    )
    any_ = pl.BlockSpec(memory_space=pl.ANY)
    vmem = pl.BlockSpec(memory_space=pltpu.VMEM)
    return pl.pallas_call(
        functools.partial(layer_kernel, (n_dp, n_z, n_x, cap, toks, width, kb, hb)),
        out_shape=jax.ShapeDtypeStruct((toks, width), BF16),
        in_specs=[vmem, vmem, vmem, pl.BlockSpec(memory_space=pltpu.SMEM), any_, any_, any_],
        out_specs=vmem,
        scratch_shapes=scratch,
        compiler_params=pltpu.CompilerParams(
            collective_id=0, has_side_effects=True, vmem_limit_bytes=60 * 2**20
        ),
    )(tokens, ids, wts, inv, gate_blocks, up_blocks, down_blocks)


def solution(mesh):
    both = ("dp", "expert")
    return jax.shard_map(
        per_device,
        mesh=mesh,
        in_specs=(
            P(both, "tensor"),
            P(both, None),
            P(both, None),
            P(both, "tensor", None),
            P(both, "tensor", None, None, None),
            P(both, "tensor", None, None, None),
            P(both, "tensor", None, None, None),
        ),
        out_specs=P(both, "tensor"),
        check_vma=False,
    )
```

time: 550 us -> 176 us (0.32)
  waiting for transfers between devices: 180 us -> 0 us
  Pallas kernels: 0 us -> 170 us
  blocking collectives: 170 us -> 0 us
  local copies, waits for them, and re-layouts: 86.6 us -> 2.25 us
  matrix products: 70.4 us -> 0 us
  starting transfers between devices: 16.1 us -> 0 us
  between operations: 13.9 us -> 0.01 us
    all_to_all x2 -> x0, blocking collectives: 170 us -> none  [the longest x1 96.9 us: per_device(): lax.all_to_all(partial_low.reshape(1, experts, capacity, D), 'tensor', sp...]
    pallas_call x0 -> x1, Pallas kernels: none -> 170 us  [per_device(): pl.pallas_call(functools.partial(layer_kernel, (n_dp, n_z, n_x, cap, toks...]
    all_to_all x1 -> x0, waiting for transfers between devices: 98.6 us -> none  [per_device(): lax.all_to_all(summed, ('dp', 'expert'), split_axis=0, concat_axis=0, til...]
    all_gather x1 -> x0, waiting for transfers between devices: 81 us -> none  [per_device(): expert_in = lax.all_gather(arrived, 'tensor', axis=2, tiled=True)]
    dot_general x10 -> x0, matrix products: 70.4 us -> none  [the longest x3 43.6 us: per_device(): jnp.einsum('rkc,kb->rbc', pieces, placer, precision=lax.Precision.HIGHEST)]
    reshape x7 -> x0, local copies, waits for them, and re-layouts: 40.1 us -> none  [the longest x2 21.6 us: per_device(): blocked = expert_in.reshape(row_count, D // BLK, BLK)]
    gather x11 -> x0, local copies, waits for them, and re-layouts: 23 us -> none  [the longest x3 12.8 us: per_device(): picked = jnp.take(blocked, chosen, axis=1)]
    all_to_all x1 -> x0, starting transfers between devices: 16.1 us -> none  [per_device(): lax.all_to_all(summed, ('dp', 'expert'), split_axis=0, concat_axis=0, til...]
  transfers between devices with their start and end apart: 2 -> 0, of which waited for: 2 -> 0; matrix products, arithmetic and copies ran while one was open for 0% -> 0% of each run, Pallas kernels for 0% -> 0%
where the time goes in v1:
time: 176 us
  Pallas kernels  170 us (97%)
  other arithmetic  3.55 us (2%)
  local copies, waits for them, and re-layouts  2.25 us (1%)
    pallas_call x1, Pallas kernels, per_device(): pl.pallas_call(functools.partial(layer_kernel, (n_dp, n_z, n_x, cap, toks...  170 us

profile of v1, /device:TPU:1, one launch (start us, length us, event | category | flops | bytes accessed | tf_op | source)
XLA Modules:
  0.0 175.7 jit_solution(2601574642090192516)
XLA Ops:
  0.0 0.7 copy.10
  0.7 0.1 select_reduce_fusion
  0.8 0.6 broadcast_add_fusion.inv
  1.4 1.4 pad_add_fusion.ids
  2.8 1.4 pad_maximum_fusion.wts
  4.2 169.9 %shard_map.73 = bf16[64,1024]{1,0:T(8,128)(2,1)} custom-call(bf16[64,1024]{1,0:T(8,128)(2,1)} %tok.1, s32[8,128]{1,0:T(8,128)} %pad_add_fusion.ids, f32[8,128]{1,0:T(8,128)} %pad_maximum_fusion.wts, s32[3,32]{1,0:T(4,128)} %broadcast_add_fusion.inv, bf16[1,3,12,128,128]{4,3,2,1,0:T(8,128)(2,1)} %gate.1, bf16[1,3,12,128,128]{4,3,2,1,0:T(8,128)(2,1)} %up.1, ...), custom_call_target="tpu_custom_call" | custom-call | tf_op jit(solution)/shard_map/pallas_call | solution.py:386
  174.1 1.6 copy.12
  (1 shorter events, 0.0 us)

commit v2 on v1

--- a/solution.py
+++ b/solution.py
@@ -1,4 +1,5 @@
 import functools
+import math
 
 import jax
 import jax.numpy as jnp
@@ -8,7 +9,7 @@
 from jax.sharding import PartitionSpec as P
 
 BLK = 128
-PIECES = 4
+PIECES = 8
 F32, BF16 = jnp.float32, jnp.bfloat16
 MESH = pl.DeviceIdType.MESH
 
@@ -17,7 +18,7 @@
     return jnp.dot(a, b, preferred_element_type=F32)
 
 
-def layer_kernel(cfg, tok, ids, wts, inv, gate, up, down, out, *scratch):
+def layer_kernel(cfg, tok, ids_ref, wts_ref, topo, gate, up, down, out, *scratch):
     n_dp, n_z, n_x, cap, toks, width, kb, hb = cfg
     (gbuf, ubuf, dbuf, gu, dn, tabs_out, tabs, tokp, zbuf, qa, va, disp, ct, comb_hi, comb_lo, ysend, xin, acc, hid,
      asend, arecv, bsend_r, bsend_l, brecv_l, brecv_r, fsend, yret, gsend, zret,
@@ -69,6 +70,8 @@
     lane = lax.broadcasted_iota(jnp.int32, (n_e, 2 * toks), 1)
     shift = n_dp.bit_length() - 1
     expert = (q & (n_dp - 1)) * n_z + (q >> shift)
+    ids = jnp.concatenate([ids_ref[...], ids_ref[...]], axis=1)
+    wts = jnp.concatenate([wts_ref[...], wts_ref[...]], axis=1)
     named = jnp.zeros((n_e, 2 * toks), F32)
     weight = jnp.zeros((n_e, 2 * toks), F32)
     for k in range(ids.shape[0]):
@@ -93,12 +96,16 @@
 
     lax.fori_loop(1, n_z, send_table, 0)
 
-    def send_tokens(j, _):
-        p, i = j // (n_z - 1), lax.rem(j, n_z - 1) + 1
-        remote(tokp.at[p], zbuf.at[p, z], z_send.at[p], z_recv.at[p], {"expert": lax.rem(z + i, n_z)}).start()
-        return 0
-
-    lax.fori_loop(0, pieces * (n_z - 1), send_tokens, 0)
+    def send_tokens(p):
+        def send(i, _):
+            to = lax.rem(z + i, n_z)
+            remote(tokp.at[p], zbuf.at[p, z], z_send.at[p], z_recv.at[p], {"expert": to}).start()
+            return 0
+
+        lax.fori_loop(1, n_z, send, 0)
+
+    send_tokens(0)
+    send_tokens(1)
     tabs[z] = tabs_out[z]
     for p in range(pieces):
         zbuf[p, z] = tokp[p]
@@ -106,21 +113,6 @@
     for buf in (gbuf, ubuf, dbuf):
         buf[:, kb] = jnp.zeros((hb, BLK, BLK), BF16)
     acc[...] = jnp.zeros(acc.shape, F32)
-    for c in weight_copies:
-        c.wait()
-
-    def dense(i, _):
-        for j in range(per):
-            b = i * per + j
-            for h in range(hb):
-                at = inv[h, b]
-                gu[i, j * BLK : (j + 1) * BLK, h * BLK : (h + 1) * BLK] = gbuf[h, at]
-                gu[i, j * BLK : (j + 1) * BLK, hid_w + h * BLK : hid_w + (h + 1) * BLK] = ubuf[h, at]
-                dn[i, h * BLK : (h + 1) * BLK, j * BLK : (j + 1) * BLK] = dbuf[h, at]
-        return 0
-
-    lax.fori_loop(0, n_x * pieces, dense, 0)
-
     drain(tabs.at[pl.ds(0, n_z - 1)], t_recv)
     low = lax.broadcasted_iota(jnp.int32, (n_dp, 2 * toks), 1) < toks
     for j in range(n_z // 2):
@@ -143,6 +135,19 @@
 
     lax.fori_loop(0, n_dp, one_hot, 0)
 
+    def dense(i, _):
+        for j in range(per):
+            b = i * per + j
+            for h in range(hb):
+                at = kb
+                for k in range(kb):
+                    at = jnp.where(topo[h, 0, k] == b, k, at)
+                gu[i, j * BLK : (j + 1) * BLK, h * BLK : (h + 1) * BLK] = gbuf[h, at]
+                gu[i, j * BLK : (j + 1) * BLK, hid_w + h * BLK : hid_w + (h + 1) * BLK] = ubuf[h, at]
+                dn[i, h * BLK : (h + 1) * BLK, j * BLK : (j + 1) * BLK] = dbuf[h, at]
+        return 0
+
+
     third = rows // 3
 
     def gather_piece(p):
@@ -180,19 +185,43 @@
         src = xin.at[right, p, pl.ds(half, half)]
         remote(src, src, l2_send.at[p], l2_recv.at[p], {"tensor": left}).start()
 
-    def add_piece(quarter, p):
-        def tile(i, _):
-            at = pl.ds(pl.multiple_of(i * third, 16), third)
-            acc[at, :] += matmul(xin[quarter, p, at, :], gu[quarter * pieces + p])
-            return 0
-
-        lax.fori_loop(0, 3, tile, 0)
+    tile = half // 2
+
+    def add_rows(quarters, p, first, tiles):
+        def add(i, _):
+            at = pl.ds(pl.multiple_of(i * tile, 16), tile)
+            acc[at, :] += sum(matmul(xin[k, p, at, :], gu[k * pieces + p]) for k in quarters)
+            return 0
+
+        lax.fori_loop(first, first + tiles, add, 0)
+
+    def split_weights():
+        tr = math.gcd(rows, BLK)
+        for j in range(rows // tr):
+            c = ct[j * tr : (j + 1) * tr, :].T
+            hi = c.astype(BF16)
+            comb_hi[:, j * tr : (j + 1) * tr] = hi
+            comb_lo[:, j * tr : (j + 1) * tr] = (c - hi.astype(F32)).astype(BF16)
 
     def inward(t, _):
         @pl.when(t < pieces)
         def _():
             gather_piece(t)
 
+        @pl.when(t + 2 < pieces)
+        def _():
+            send_tokens(t + 2)
+
+        @pl.when(t == 0)
+        def _():
+            for c in weight_copies:
+                c.wait()
+            lax.fori_loop(0, n_x * pieces, dense, 0)
+
+        @pl.when(t == 1)
+        def _():
+            split_weights()
+
         @pl.when((t >= 1) & (t < pieces + 1))
         def _():
             spread_piece(t - 1)
@@ -200,45 +229,40 @@
         @pl.when((t >= 2) & (t < pieces + 2))
         def _():
             forward_piece(t - 2)
-            add_piece(x, t - 2)
-            add_piece(left, t - 2)
-            add_piece(right, t - 2)
+            add_rows((x, left, right), t - 2, 0, 4)
 
         @pl.when(t >= 3)
         def _():
             drain(xin.at[far, t - 3, pl.ds(0, half)], r2_recv.at[t - 3])
             drain(xin.at[far, t - 3, pl.ds(half, half)], l2_recv.at[t - 3])
-            add_piece(far, t - 3)
-
-        return 0
-
-    tr = min(rows, BLK)
-    for j in range(rows // tr):
-        c = ct[j * tr : (j + 1) * tr, :].T
-        hi = c.astype(BF16)
-        comb_hi[:, j * tr : (j + 1) * tr] = hi
-        comb_lo[:, j * tr : (j + 1) * tr] = (c - hi.astype(F32)).astype(BF16)
-
-    lax.fori_loop(0, pieces + 3, inward, 0)
+            add_rows((far,), t - 3, 0, 4)
+
+        return 0
+
+    lax.fori_loop(0, pieces + 2, inward, 0)
 
     def activate(i, _):
-        at = pl.ds(pl.multiple_of(i * third, 16), third)
+        at = pl.ds(pl.multiple_of(i * tile, 16), tile)
         g = acc[at, :hid_w]
         hid[at, :] = (g / (1.0 + jnp.exp(-g)) * acc[at, hid_w:]).astype(BF16)
         return 0
 
-    lax.fori_loop(0, 3, activate, 0)
-
     def partial(quarter, p, part):
         return matmul(hid[part * half : (part + 1) * half, :], dn[quarter * pieces + p])
 
     lo, hi_ = pl.ds(0, half), pl.ds(half, half)
 
-    def send_far(p):
+    def send_far_lo(p):
         asend[p, lo, :] = partial(far, p, 0).astype(BF16)
         remote(asend.at[p, lo], arecv.at[p, lo], ar_send.at[p], ar_recv.at[p], {"tensor": right}).start()
+
+    def send_far_hi(p):
         asend[p, hi_, :] = partial(far, p, 1).astype(BF16)
         remote(asend.at[p, hi_], arecv.at[p, hi_], al_send.at[p], al_recv.at[p], {"tensor": left}).start()
+
+    def send_far(p):
+        send_far_lo(p)
+        send_far_hi(p)
 
     def send_near(p):
         bsend_r[p, hi_, :] = partial(right, p, 1).astype(BF16)
@@ -293,52 +317,64 @@
             total = total + zret[p, h].astype(F32)
         out[:, pl.ds(pl.multiple_of(p * w, BLK), w)] = total.astype(BF16)
 
-    send_far(0)
-    send_far(1)
-
-    def outward(t, _):
-        @pl.when(t < pieces)
-        def _():
-            send_near(t)
-
-        @pl.when(t + 2 < pieces)
-        def _():
-            send_far(t + 2)
-
-        @pl.when((t >= 1) & (t < pieces + 1))
-        def _():
-            send_home(t - 1)
-
-        @pl.when((t >= 2) & (t < pieces + 2))
-        def _():
-            combine(t - 2)
-
-        @pl.when(t >= 3)
-        def _():
-            finish(t - 3)
-
-        return 0
-
-    lax.fori_loop(0, pieces + 3, outward, 0)
-
-    drain(tabs_out.at[pl.ds(0, n_z - 1)], t_send)
-
-    def settle(p, _):
+    def settle_inward(p):
         drain(zbuf.at[p, pl.ds(0, n_z - 1)], z_send.at[p])
         drain(ysend.at[p, pl.ds(0, rows - grp)], y_send.at[p])
         drain(xin.at[0, p], r1_send.at[p])
         drain(xin.at[0, p], l1_send.at[p])
         drain(xin.at[0, p, lo], r2_send.at[p])
         drain(xin.at[0, p, lo], l2_send.at[p])
+
+    last = pieces - 1
+    drain(xin.at[far, last, lo], r2_recv.at[last])
+    add_rows((far,), last, 0, 2)
+    lax.fori_loop(0, 2, activate, 0)
+    send_far_lo(0)
+    drain(xin.at[far, last, hi_], l2_recv.at[last])
+    add_rows((far,), last, 2, 2)
+    lax.fori_loop(2, 4, activate, 0)
+    send_far_hi(0)
+    send_far(1)
+    send_far(2)
+
+    def settle_outward(p):
         drain(asend.at[p, lo], ar_send.at[p])
         drain(asend.at[p, lo], al_send.at[p])
         drain(bsend_r.at[p], br_send.at[p])
         drain(bsend_l.at[p], bl_send.at[p])
         drain(fsend.at[p, pl.ds(0, rows - grp)], f_send.at[p])
         drain(gsend.at[p, pl.ds(0, n_z - 1)], g_send.at[p])
-        return 0
-
-    lax.fori_loop(0, pieces, settle, 0)
+
+    def outward(t, _):
+        @pl.when(t < pieces)
+        def _():
+            send_near(t)
+
+        @pl.when(t + 3 < pieces)
+        def _():
+            send_far(t + 3)
+
+        @pl.when((t >= 1) & (t < pieces + 1))
+        def _():
+            send_home(t - 1)
+
+        @pl.when((t >= 2) & (t < pieces + 2))
+        def _():
+            combine(t - 2)
+
+        @pl.when(t < pieces)
+        def _():
+            settle_inward(t)
+
+        @pl.when(t >= 3)
+        def _():
+            finish(t - 3)
+            settle_outward(t - 3)
+
+        return 0
+
+    lax.fori_loop(0, pieces + 3, outward, 0)
+    drain(tabs_out.at[pl.ds(0, n_z - 1)], t_send)
 
 
 def per_device(tokens, expert_ids, combine_weights, topology, gate_blocks, up_blocks, down_blocks):
@@ -347,13 +383,8 @@
     top = expert_ids.shape[1]
     cap = min(toks, 3 * toks * top // (2 * n_dp * n_z))
     _, hb, kb = topology.shape
-    n_b = n_x * width // BLK
     pieces, w = PIECES, width // PIECES
     rows, grp = n_dp * n_z * cap, n_z * cap
-    ids = jnp.concatenate([expert_ids.T, expert_ids.T], axis=1)
-    wts = jnp.concatenate([combine_weights.T, combine_weights.T], axis=1)
-    hits = topology[0][:, :, None] == jnp.arange(n_b, dtype=jnp.int32)[None, None, :]
-    inv = kb + jnp.sum(jnp.where(hits, jnp.arange(kb, dtype=jnp.int32)[None, :, None] - kb, 0), axis=1)
     vm, dma = pltpu.VMEM, pltpu.SemaphoreType.DMA
     hid_w = hb * BLK
     scratch = (
@@ -392,7 +423,7 @@
         compiler_params=pltpu.CompilerParams(
             collective_id=0, has_side_effects=True, vmem_limit_bytes=60 * 2**20
         ),
-    )(tokens, ids, wts, inv, gate_blocks, up_blocks, down_blocks)
+    )(tokens, expert_ids.T, combine_weights.T, topology.transpose(1, 0, 2), gate_blocks, up_blocks, down_blocks)
 
 
 def solution(mesh):

time: 176 us -> 160 us (0.909)
  Pallas kernels: 170 us -> 158 us
  other arithmetic: 3.55 us -> 0 us
    pallas_call x1, Pallas kernels: 170 us -> 158 us  [per_device(): pl.pallas_call(functools.partial(layer_kernel, (n_dp, n_z, n_x, cap, toks...]
    concatenate x2 -> x0, other arithmetic: 2.85 us -> none  [the longest x1 1.43 us: per_device(): ids = jnp.concatenate([expert_ids.T, expert_ids.T], axis=1)]
where the time goes in v2:
time: 160 us
  Pallas kernels  158 us (99%)
    pallas_call x1, Pallas kernels, per_device(): pl.pallas_call(functools.partial(layer_kernel, (n_dp, n_z, n_x, cap, toks...  158 us

profile of v2, /device:TPU:1, one launch (start us, length us, event | category | flops | bytes accessed | tf_op | source)
XLA Modules:
  0.0 159.7 jit_solution(3360628893110533829)
XLA Ops:
  0.0 158.1 %shard_map.73 = bf16[64,1024]{1,0:T(8,128)(2,1)} custom-call(bf16[64,1024]{1,0:T(8,128)(2,1)} %tok.1, s32[8,64]{1,0:T(8,128)} %bitcast.3, f32[8,64]{1,0:T(8,128)} %bitcast.4, s32[3,1,12]{2,1,0:T(1,128)} %bitcast.5, bf16[1,3,12,128,128]{4,3,2,1,0:T(8,128)(2,1)} %gate.1, bf16[1,3,12,128,128]{4,3,2,1,0:T(8,128)(2,1)} %up.1, bf16[1,3,12,128,128]{4,3,2,1,0:T(8,128)(2,1)} %down.1), custom_call_target="tpu_custom_call" | custom-call | tf_op jit(solution)/shard_map/pallas_call | solution.py:417
  158.2 1.6 copy.9
